TPU v7x, 32 devices: a whole 2x2x4 slice. The times are simulated.
32 devices in a mesh: dp: 8 (over y, x, core), mp: 4 (over z).
Axes of the slice: x: 2, y: 2, z: 4, core: 2. Of those that a mesh axis runs over, the one named last changes fastest.
Arguments:
- tokens: bfloat16 [64, 256, 1024], P(('dp', 'mp')), may hold values from -6 to 6
- cotangent: bfloat16 [64, 256, 1024], P(('dp', 'mp')), may hold values from -6 to 6
- w_qkv: bfloat16 [3, 1024, 1024], P(None, None, 'mp'), may hold values from -0.1875 to 0.1875
- w_out: bfloat16 [1024, 1024], P('mp'), may hold values from -1 to 1
- w_up: bfloat16 [1024, 4096], P(None, 'mp'), may hold values from -0.1875 to 0.1875
- w_down: bfloat16 [4096, 1024], P('mp'), may hold values from -0.09375 to 0.09375
- w_mod: bfloat16 [1024, 6144], P('mp'), may hold values from -0.1875 to 0.1875
- b_mod: bfloat16 [6, 1024], replicated, may hold values from -3 to 3
- time_weight: bfloat16 [256, 1024], P(None, 'mp'), may hold values from -0.375 to 0.375
- class_table: bfloat16 [1000, 1024], P(None, 'mp'), may hold values from -6 to 6
- rel_table: bfloat16 [16, 961], P('mp'), may hold values from -5 to 5
- window_step: int32 [64], P('dp'), may hold values from 0 to 999
- window_label: int32 [64], P('dp'), may hold values from 0 to 999
- window_cols: int32 [64], P('dp'), may hold values from 0 to 16, as said below
Outputs:
- block_out: bfloat16 [64, 256, 1024], P(('dp', 'mp'))
- tokens_grad: bfloat16 [64, 256, 1024], P(('dp', 'mp'))
- w_qkv_grad: float32 [3, 1024, 1024], P(None, None, 'mp')
- w_out_grad: float32 [1024, 1024], P('mp')
- w_up_grad: float32 [1024, 4096], P(None, 'mp')
- w_down_grad: float32 [4096, 1024], P('mp')
- w_mod_grad: float32 [1024, 6144], P('mp')
- b_mod_grad: float32 [6, 1024], replicated
- time_weight_grad: float32 [256, 1024], P(None, 'mp')
- class_table_grad: float32 [1000, 1024], P(None, 'mp')
- rel_table_grad: float32 [16, 961], P('mp')
Inputs may be any that keep to these rules, and one draw needn't show every extreme that they name: `window_cols`: within each aligned block of 8 windows the used slots (nonzero entry) come first, two or more of them; some block is used in full. A used slot holds 16 or 8 valid columns, an unused one 0.
All inputs are finite; a program needn't handle non-finite values.
Results may differ from a plain program's by a relative error of at most 0.028.
Values may be sent and summed in bfloat16 or wider, within the bound.
No kernel may reach another device: no remote copies, remote signals or barrier semaphores. Data moves between devices by JAX's collectives and lax.ppermute only.
A program may use at most 192 MiB of HBM per device.

v0:
```python
import math
import jax
import jax.numpy as jnp
from jax import lax
from jax.sharding import PartitionSpec as P

HEAD_DIM = 64
WSIDE = 16
FREQ = 256
EPS = 1e-06
HIGH = lax.Precision.HIGHEST
MASKED = -1000000000.0


def exact(matrix_a, matrix_b):
    return jnp.dot(matrix_a, matrix_b, precision=HIGH, preferred_element_type=jnp.float32)


def layer_norm(field):
    center = field - jnp.mean(field, axis=-1, keepdims=True)
    spread = jnp.mean(center * center, axis=-1, keepdims=True)
    return center * lax.rsqrt(spread + EPS)


def modulate(field, scale_part, shift_part):
    return layer_norm(field) * (1.0 + scale_part) + shift_part


def gelu_tanh(field):
    return jax.nn.gelu(field, approximate=True)


def step_features(step_ids, half_width):
    frequency = jnp.exp(-math.log(10000.0) * jnp.arange(half_width, dtype=jnp.float32) / half_width)
    angles = step_ids.astype(jnp.float32)[:, None] * frequency[None, :]
    return jnp.concatenate([jnp.cos(angles), jnp.sin(angles)], axis=1)


def offset_table(window_side):
    offsets = jnp.arange(window_side, dtype=jnp.int32)
    offset_diff = offsets[:, None] - offsets[None, :] + window_side - 1
    return (
        offset_diff[None] == jnp.arange(2 * window_side - 1, dtype=jnp.int32)[:, None, None]
    ).astype(jnp.float32)


def make_scores(queries, keys, rel_bias, keep_keys, score_scale):
    raw_scores = (
        jnp.einsum("wihd,wjhd->whij", queries, keys, preferred_element_type=jnp.float32)
        * score_scale
        + rel_bias[None]
    )
    return jnp.where(keep_keys[:, None, None, :], raw_scores, MASKED)


def per_device(
    tokens,
    cotangent,
    w_qkv,
    w_out,
    w_up,
    w_down,
    w_mod,
    b_mod,
    time_weight,
    class_table,
    rel_table,
    window_step,
    window_label,
    window_cols,
):
    own_count, win_tok, width = tokens.shape
    group_size = window_step.shape[0]
    local_heads = w_out.shape[0] // HEAD_DIM
    score_scale = HEAD_DIM ** (-0.5)
    first_own = lax.axis_index("mp") * own_count
    features = step_features(window_step, FREQ // 2).astype(jnp.bfloat16)
    classes = jnp.arange(class_table.shape[0], dtype=jnp.int32)
    onehot = (window_label[:, None] == classes[None, :]).astype(jnp.bfloat16)
    cond_pre = jnp.dot(features, time_weight, preferred_element_type=jnp.float32) + jnp.dot(
        onehot, class_table, preferred_element_type=jnp.float32
    )
    condition = jax.nn.silu(cond_pre).astype(jnp.bfloat16)
    partial_mod = jnp.dot(condition, w_mod, preferred_element_type=jnp.float32)
    modulation = (
        lax.psum(partial_mod, "mp").reshape(group_size, 6, width) + b_mod.astype(jnp.float32)[None]
    )
    own_mod = lax.dynamic_slice_in_dim(modulation, first_own, own_count, 0)
    shift_attn, scale_attn, gate_attn, shift_mlp, scale_mlp, gate_mlp = [
        own_mod[:, column][:, None, :] for column in range(6)
    ]
    token_cols = jnp.arange(win_tok, dtype=jnp.int32) % WSIDE
    keep_keys = token_cols[None, :] < window_cols[:, None]
    keep_rows = lax.dynamic_slice_in_dim(keep_keys, first_own, own_count, 0)[:, :, None]
    rel_span = 2 * WSIDE - 1
    offset_pick = offset_table(WSIDE)
    rel_grid = rel_table.astype(jnp.float32).reshape(local_heads, rel_span, rel_span)
    half_bias = jnp.einsum("ayz,hab->hyzb", offset_pick, rel_grid, precision=HIGH)
    rel_bias = jnp.einsum("hyzb,bxw->hyxzw", half_bias, offset_pick, precision=HIGH).reshape(
        local_heads, win_tok, win_tok
    )
    inputs = tokens.astype(jnp.float32)
    normed_attn = modulate(inputs, scale_attn, shift_attn).astype(jnp.bfloat16)
    gathered_attn = lax.all_gather(normed_attn, "mp", axis=0, tiled=True)
    projected = jnp.einsum(
        "wtd,kde->kwte", gathered_attn, w_qkv, preferred_element_type=jnp.float32
    ).astype(jnp.bfloat16)
    split_shape = (group_size, win_tok, local_heads, HEAD_DIM)
    queries = projected[0].reshape(split_shape)
    keys = projected[1].reshape(split_shape)
    values = projected[2].reshape(split_shape)
    scores = make_scores(queries, keys, rel_bias, keep_keys, score_scale)
    row_max = jnp.max(scores, axis=-1, keepdims=True)
    log_total = row_max + jnp.log(jnp.sum(jnp.exp(scores - row_max), axis=-1, keepdims=True))
    probs_low = jnp.exp(scores - log_total).astype(jnp.bfloat16)
    attended = (
        jnp.einsum("whij,wjhd->wihd", probs_low, values, preferred_element_type=jnp.float32)
        .astype(jnp.bfloat16)
        .reshape(group_size, win_tok, local_heads * HEAD_DIM)
    )
    row_block = attended
    branch = lax.psum_scatter(
        jnp.einsum("wte,ed->wtd", row_block, w_out, preferred_element_type=jnp.float32).astype(
            jnp.bfloat16
        ),
        "mp",
        scatter_dimension=0,
        tiled=True,
    ).astype(jnp.float32)
    middle = inputs + gate_attn * branch
    normed_mlp = modulate(middle, scale_mlp, shift_mlp).astype(jnp.bfloat16)
    gathered_mlp = lax.all_gather(normed_mlp, "mp", axis=0, tiled=True)
    hidden_pre = jnp.einsum("wtd,df->wtf", gathered_mlp, w_up, preferred_element_type=jnp.float32)
    activation = gelu_tanh(hidden_pre).astype(jnp.bfloat16)
    row_block = activation
    mlp_out = lax.psum_scatter(
        jnp.einsum("wtf,fd->wtd", row_block, w_down, preferred_element_type=jnp.float32).astype(
            jnp.bfloat16
        ),
        "mp",
        scatter_dimension=0,
        tiled=True,
    ).astype(jnp.float32)
    block_out = jnp.where(keep_rows, middle + gate_mlp * mlp_out, 0.0).astype(jnp.bfloat16)
    grad_rows = jnp.where(keep_rows, cotangent.astype(jnp.float32), 0.0)
    d_gate_mlp = jnp.sum(grad_rows * mlp_out, axis=1)
    d_mlp = (gate_mlp * grad_rows).astype(jnp.bfloat16)
    d_mlp_all = lax.all_gather(d_mlp, "mp", axis=0, tiled=True)
    normed_again = lax.all_gather(normed_mlp, "mp", axis=0, tiled=True)
    pre_again = jnp.einsum("wtd,df->wtf", normed_again, w_up, preferred_element_type=jnp.float32)
    act_again = gelu_tanh(pre_again).astype(jnp.bfloat16)
    w_down_grad = jnp.einsum(
        "wtf,wtd->fd", act_again, d_mlp_all, preferred_element_type=jnp.float32
    )
    d_act = jnp.einsum("wtd,fd->wtf", d_mlp_all, w_down, preferred_element_type=jnp.float32)
    d_hidden = jax.vjp(gelu_tanh, pre_again)[1](d_act)[0].astype(jnp.bfloat16)
    w_up_grad = jnp.einsum(
        "wtd,wtf->df", normed_again, d_hidden, preferred_element_type=jnp.float32
    )
    row_block = d_hidden
    d_normed_mlp = lax.psum_scatter(
        jnp.einsum("wtf,df->wtd", row_block, w_up, preferred_element_type=jnp.float32),
        "mp",
        scatter_dimension=0,
        tiled=True,
    )
    pull_mlp = jax.vjp(modulate, middle, scale_mlp, shift_mlp)[1]
    d_middle_norm, d_scale_mlp, d_shift_mlp = pull_mlp(d_normed_mlp)
    d_middle = grad_rows + d_middle_norm
    d_gate_attn = jnp.sum(d_middle * branch, axis=1)
    d_branch = (gate_attn * d_middle).astype(jnp.bfloat16)
    d_branch_all = lax.all_gather(d_branch, "mp", axis=0, tiled=True)
    w_out_grad = jnp.einsum(
        "wte,wtd->ed", attended, d_branch_all, preferred_element_type=jnp.float32
    )
    d_attended = (
        jnp.einsum("wtd,ed->wte", d_branch_all, w_out, preferred_element_type=jnp.float32)
        .astype(jnp.bfloat16)
        .reshape(split_shape)
    )
    probs_back = jnp.exp(make_scores(queries, keys, rel_bias, keep_keys, score_scale) - log_total)
    d_probs = jnp.einsum("wihd,wjhd->whij", d_attended, values, preferred_element_type=jnp.float32)
    d_values = jnp.einsum(
        "whij,wihd->wjhd",
        probs_back.astype(jnp.bfloat16),
        d_attended,
        preferred_element_type=jnp.float32,
    ).astype(jnp.bfloat16)
    row_delta = jnp.sum(probs_back * d_probs, axis=-1, keepdims=True)
    d_scores = (probs_back * (d_probs - row_delta)).astype(jnp.bfloat16)
    d_queries = (
        jnp.einsum("whij,wjhd->wihd", d_scores, keys, preferred_element_type=jnp.float32)
        * score_scale
    ).astype(jnp.bfloat16)
    d_keys = (
        jnp.einsum("whij,wihd->wjhd", d_scores, queries, preferred_element_type=jnp.float32)
        * score_scale
    ).astype(jnp.bfloat16)
    d_bias = jnp.sum(d_scores, axis=0, dtype=jnp.float32).reshape(
        local_heads, WSIDE, WSIDE, WSIDE, WSIDE
    )
    d_half = jnp.einsum("hyxzw,bxw->hyzb", d_bias, offset_pick, precision=HIGH)
    rel_table_grad = jnp.einsum("hyzb,ayz->hab", d_half, offset_pick, precision=HIGH).reshape(
        local_heads, rel_span * rel_span
    )
    d_projected = jnp.stack([d_queries, d_keys, d_values]).reshape(
        3, group_size, win_tok, local_heads * HEAD_DIM
    )
    w_qkv_grad = jnp.einsum(
        "wtd,kwte->kde", gathered_attn, d_projected, preferred_element_type=jnp.float32
    )
    row_block = d_projected
    d_normed_attn = lax.psum_scatter(
        jnp.einsum("kwte,kde->wtd", row_block, w_qkv, preferred_element_type=jnp.float32).astype(
            jnp.bfloat16
        ),
        "mp",
        scatter_dimension=0,
        tiled=True,
    ).astype(jnp.float32)
    pull_attn = jax.vjp(modulate, inputs, scale_attn, shift_attn)[1]
    d_inputs_norm, d_scale_attn, d_shift_attn = pull_attn(d_normed_attn)
    tokens_grad = (d_middle + d_inputs_norm).astype(jnp.bfloat16)
    d_mod_own = jnp.stack(
        [
            d_shift_attn[:, 0],
            d_scale_attn[:, 0],
            d_gate_attn,
            d_shift_mlp[:, 0],
            d_scale_mlp[:, 0],
            d_gate_mlp,
        ],
        axis=1,
    ).reshape(own_count, 6 * width)
    d_modulation = lax.all_gather(d_mod_own.astype(jnp.bfloat16), "mp", axis=0, tiled=True).astype(
        d_mod_own.dtype
    )
    d_condition = exact(d_modulation, w_mod.T)
    d_cond_pre = jax.vjp(jax.nn.silu, cond_pre)[1](d_condition)[0]
    time_weight_grad = exact(features.astype(jnp.float32).T, d_cond_pre)
    class_table_grad = exact(onehot.astype(jnp.float32).T, d_cond_pre)
    w_mod_grad = exact(condition.astype(jnp.float32).T, d_modulation)
    b_mod_grad = jnp.sum(d_modulation, axis=0).reshape(6, width)
    (
        w_qkv_grad,
        w_out_grad,
        w_up_grad,
        w_down_grad,
        w_mod_grad,
        b_mod_grad,
        time_weight_grad,
        class_table_grad,
        rel_table_grad,
    ) = lax.psum(
        (
            w_qkv_grad,
            w_out_grad,
            w_up_grad,
            w_down_grad,
            w_mod_grad,
            b_mod_grad,
            time_weight_grad,
            class_table_grad,
            rel_table_grad,
        ),
        "dp",
    )
    return (
        block_out,
        tokens_grad,
        w_qkv_grad,
        w_out_grad,
        w_up_grad,
        w_down_grad,
        w_mod_grad,
        b_mod_grad,
        time_weight_grad,
        class_table_grad,
        rel_table_grad,
    )


def solution(mesh):
    return jax.shard_map(
        per_device,
        mesh=mesh,
        in_specs=(
            P(("dp", "mp"), None, None),
            P(("dp", "mp"), None, None),
            P(None, None, "mp"),
            P("mp", None),
            P(None, "mp"),
            P("mp", None),
            P("mp", None),
            P(),
            P(None, "mp"),
            P(None, "mp"),
            P("mp", None),
            P("dp"),
            P("dp"),
            P("dp"),
        ),
        out_specs=(
            P(("dp", "mp"), None, None),
            P(("dp", "mp"), None, None),
            P(None, None, "mp"),
            P("mp", None),
            P(None, "mp"),
            P("mp", None),
            P("mp", None),
            P(),
            P(None, "mp"),
            P(None, "mp"),
            P("mp", None),
        ),
        check_vma=False,
    )
```

profile of v0, /device:TPU:0, one launch (start us, length us, event | category | flops | bytes accessed | tf_op | source)
XLA Modules:
  0.0 1149.7 jit_solution(5632088591709699951)
XLA Ops:
  14.9 34.8 %all-reduce.5.cloned.1.call-done = f32[8,6,1024]{2,0,1:T(8,128)} async-done(((f32[8,6,1024]{2,0,1:T(8,128)}), f32[8,6,1024]{2,0,1:T(8,128)}) %all-reduce.5.cloned.1.call-update) | async-done | bytes 196624 | tf_op jit(solution)/shard_map/psum | solution.py:86
  54.1 5.6 convolution_bitcast_fusion
  59.8 12.0 %copy.103 = f32[4,16,16,16,16]{2,1,4,3,0:T(8,128)} copy(f32[4,16,16,16,16]{3,4,1,0,2:T(8,128)} %convolution_bitcast_fusion) | data formatting | bytes 2097152 | tf_op jit(solution)/shard_map/add | solution.py:49
  71.8 7.0 reshape.213
  78.9 55.0 %all-gather.6.cloned.1.call-done = bf16[8,256,1024]{2,1,0:T(8,128)(2,1)} async-done(((bf16[2,256,1024]{2,1,0:T(8,128)(2,1)}), bf16[8,256,1024]{2,1,0:T(8,128)(2,1)}) %all-gather.6.cloned.1.call-update) | async-done | bytes 4194320 | tf_op jit(solution)/shard_map/all_gather | solution.py:104
  133.9 6.1 convert_bitcast_fusion
  153.3 75.4 %reduce-scatter.5.cloned.1.call-done = bf16[2,256,1024]{2,1,0:T(8,128)(2,1)} async-done(((bf16[8,256,1024]{2,1,0:T(8,128)(2,1)}), bf16[2,256,1024]{2,1,0:T(8,128)(2,1)}) %reduce-scatter.5.cloned.1.call-update) | async-done | bytes 1048592 | tf_op jit(solution)/shard_map/reduce_scatter | solution.py:122
  237.2 78.7 %all-gather.8.cloned.1.call-done = bf16[8,256,1024]{2,1,0:T(8,128)(2,1)} async-done(((bf16[2,256,1024]{2,1,0:T(8,128)(2,1)}), bf16[8,256,1024]{2,1,0:T(8,128)(2,1)}) %all-gather.8.cloned.1.call-update) | async-done | bytes 4194320 | tf_op jit(solution)/shard_map/all_gather | solution.py:132
  316.0 10.9 fusion.34
  326.9 70.4 %all-gather.10.cloned.1.call-done = bf16[8,256,1024]{2,1,0:T(8,128)(2,1)} async-done(((bf16[2,256,1024]{2,1,0:T(8,128)(2,1)}), bf16[8,256,1024]{2,1,0:T(8,128)(2,1)}) %all-gather.10.cloned.1.call-update) | async-done | bytes 4194320 | tf_op jit(solution)/shard_map/all_gather | solution.py:148
  397.2 12.8 %fusion.6 = bf16[8,256,1024]{2,1,0:T(8,128)(2,1)S(1)} fusion(f32[8,256,1024]{2,1,0:T(8,128)} %fusion.34, bf16[8,256,1024]{2,1,0:T(8,128)(2,1)} %all-gather.10.cloned.1.call-done, bf16[1024,1024]{1,0:T(8,128)(2,1)} %param.19), kind=kOutput, calls=%fused_computation.8 | convolution fusion | flops 4336910336 | bytes 18874368 | tf_op jit(solution)/shard_map/wtd,fd->wtf/dot_general | solution.py:155
  412.0 7.0 fusion.32
  419.1 143.2 %reduce-scatter.9.cloned.1.call-done = f32[2,256,1024]{2,1,0:T(8,128)} async-done(((f32[8,256,1024]{2,1,0:T(8,128)}), f32[2,256,1024]{2,1,0:T(8,128)}) %reduce-scatter.9.cloned.1.call-update) | async-done | bytes 2097168 | tf_op jit(solution)/shard_map/reduce_scatter | solution.py:161
  569.6 81.5 %all-gather.12.cloned.1.call-done = bf16[8,256,1024]{2,1,0:T(8,128)(2,1)} async-done(((bf16[2,256,1024]{2,1,0:T(8,128)(2,1)}), bf16[8,256,1024]{2,1,0:T(8,128)(2,1)}) %all-gather.12.cloned.1.call-update) | async-done | bytes 4194320 | tf_op jit(solution)/shard_map/all_gather | solution.py:172
  651.0 3.7 convolution_convert_fusion.3
  654.8 6.0 convolution_convert_fusion.2
  663.3 3.9 convert_reduce_fusion
  678.1 7.8 bitcast_convert_fusion
  686.0 11.5 %convolution_convert_fusion = bf16[8,256,1024]{2,1,0:T(8,128)(2,1)} fusion(bf16[1024,1024]{1,0:T(8,128)(2,1)} %param.19, f32[8,256,1024]{2,1,0:T(8,128)} %fusion.34), kind=kOutput, calls=%fused_computation.34 | convolution fusion | flops 4315938816 | bytes 14680064 | tf_op jit(solution)/shard_map/wtf,fd->wtd/dot_general | solution.py:137
  697.8 10.2 convolution_bitcast_fusion.2
  708.1 11.2 convolution_bitcast_fusion.1
  722.8 5.5 fusion.36
  728.3 33.1 %reduce-scatter.11.cloned.1.call-done = bf16[2,256,1024]{2,1,0:T(8,128)(2,1)} async-done(((bf16[8,256,1024]{2,1,0:T(8,128)(2,1)}), bf16[2,256,1024]{2,1,0:T(8,128)(2,1)}) %reduce-scatter.11.cloned.1.call-update) | async-done | bytes 1048592 | tf_op jit(solution)/shard_map/reduce_scatter | solution.py:213
  767.7 74.0 %reduce-scatter.7.cloned.1.call-done = bf16[2,256,1024]{2,1,0:T(8,128)(2,1)} async-done(((bf16[8,256,1024]{2,1,0:T(8,128)(2,1)}), bf16[2,256,1024]{2,1,0:T(8,128)(2,1)}) %reduce-scatter.7.cloned.1.call-update) | async-done | bytes 1048592 | tf_op jit(solution)/shard_map/reduce_scatter | solution.py:136
  841.6 5.2 fusion.26
  847.0 13.8 %all-gather = bf16[4,2,6144]{2,1,0:T(2,128)(2,1)S(1)} all-gather(bf16[1,2,6144]{2,1,0:T(2,128)(2,1)S(1)} %bitcast.178), channel_id=1, replica_groups=mesh['dp'=8,'mp'=4] {'mp'}, dimensions={0}, use_global_device_ids=true | all-gather | bytes 122880 | tf_op jit(solution)/shard_map/all_gather | solution.py:235
  864.4 3.7 fusion.77
  869.0 6.2 reshape.189
  875.2 6.8 convolution_bitcast_fusion.5
  882.7 25.6 %all-reduce = (f32[6,1024]{1,0:T(8,128)}, f32[4,961]{1,0:T(4,128)}) all-reduce(f32[6,1024]{1,0:T(8,128)S(1)} %reshape.188, f32[4,961]{1,0:T(4,128)S(1)} %reshape.190), channel_id=1, replica_groups=mesh['dp'=8,'mp'=4] {'dp'}, use_global_device_ids=true, to_apply=%region_28.29 | all-reduce | flops 9988 | bytes 79904 | tf_op jit(solution)/shard_map/psum | solution.py:254
  908.3 215.6 %all-reduce.7.cloned.1.call-done = (f32[3,1024,256]{1,2,0:T(8,128)}, f32[256,1024]{1,0:T(8,128)}, f32[1024,1024]{1,0:T(8,128)}, f32[1024,1024]{1,0:T(8,128)}, f3...) async-done(((f32[3,1024,256]{1,2,0:T(8,128)}, f32[256,1024]{1,0:T(8,128)}, f32[1024,1024]{1,0:T(8,128)}, f32[1024,1024]{1,0:T(8,128)}, ...) | async-done | bytes 20160528 | tf_op jit(solution)/shard_map/psum | solution.py:254
  1129.7 5.1 copy.125
  (172 shorter events, 85.5 us)
Async XLA Ops:
  7.2 42.5 %all-reduce.5.cloned.1.call-start = ((), (), s32[]{:S(2)}) async-start(), calls=%async_computation.4 | async-start | bytes 393216 | tf_op jit(solution)/shard_map/psum | solution.py:86
  8.2 6.7 copy-start.27
  11.7 41.7 %copy-start.28 = (bf16[4,961]{1,0:T(4,128)(2,1)S(1)}, bf16[4,961]{1,0:T(4,128)(2,1)}, u32[]{:S(2)}) copy-start(bf16[4,961]{1,0:T(4,128)(2,1)} %param.24) | copy-start | bytes 23068
  11.7 122.2 %all-gather.6.cloned.1.call-start = ((), (), s32[]{:S(2)}) async-start(), calls=%async_computation.5 | async-start | bytes 5242880 | tf_op jit(solution)/shard_map/all_gather | solution.py:104
  53.3 175.4 %reduce-scatter.5.cloned.1.call-start = ((), (), s32[]{:S(2)}) async-start(), calls=%async_computation.6 | async-start | bytes 5242880 | tf_op jit(solution)/shard_map/reduce_scatter | solution.py:122
  71.8 7.0 copy-start.30
  140.3 4.0 copy-start.7
  140.3 4.0 copy-start.12
  140.3 5.7 copy-start.9
  153.3 162.7 %all-gather.8.cloned.1.call-start = ((), (), s32[]{:S(2)}) async-start(), calls=%async_computation.7 | async-start | bytes 5242880 | tf_op jit(solution)/shard_map/all_gather | solution.py:132
  228.7 4.2 copy-start.2
  228.7 4.2 copy-start.4
  234.6 162.6 %all-gather.10.cloned.1.call-start = ((), (), s32[]{:S(2)}) async-start(), calls=%async_computation.9 | async-start | bytes 5242880 | tf_op jit(solution)/shard_map/all_gather | solution.py:148
  237.2 325.1 %reduce-scatter.9.cloned.1.call-start = ((), (), s32[]{:S(2)}) async-start(), calls=%async_computation.10 | async-start | bytes 10485760 | tf_op jit(solution)/shard_map/reduce_scatter | solution.py:161
  397.2 14.8 %copy-start.34 = (bf16[1024,1024]{1,0:T(8,128)(2,1)S(1)}, bf16[1024,1024]{1,0:T(8,128)(2,1)}, u32[]{:S(2)}) copy-start(bf16[1024,1024]{1,0:T(8,128)(2,1)} %param.18) | copy-start | bytes 6291460
  419.0 232.0 %all-gather.12.cloned.1.call-start = ((), (), s32[]{:S(2)}) async-start(), calls=%async_computation.11 | async-start | bytes 5242880 | tf_op jit(solution)/shard_map/all_gather | solution.py:172
  562.3 3.5 copy-start.14
  569.5 191.9 %reduce-scatter.11.cloned.1.call-start = ((), (), s32[]{:S(2)}) async-start(), calls=%async_computation.12 | async-start | bytes 5242880 | tf_op jit(solution)/shard_map/reduce_scatter | solution.py:213
  651.0 9.7 slice-start
  654.8 6.0 slice-start.1
  654.8 6.0 copy-start.10
  663.3 3.9 copy-start.13
  686.0 155.7 %reduce-scatter.7.cloned.1.call-start = ((), (), s32[]{:S(2)}) async-start(), calls=%async_computation.8 | async-start | bytes 5242880 | tf_op jit(solution)/shard_map/reduce_scatter | solution.py:136
  697.6 426.2 %all-reduce.7.cloned.1.call-start = ((), (), s32[]{:S(2)}) async-start(), calls=%async_computation.13 | async-start | bytes 40321024 | tf_op jit(solution)/shard_map/psum | solution.py:254
  697.8 10.2 copy-start.32
  708.1 11.2 copy-start.18
  708.1 11.2 copy-start.33
  719.3 3.6 copy-start.31
  846.9 15.9 %copy-start.29 = (s32[8]{0:T(128)S(1)}, s32[8]{0:T(128)}, u32[]{:S(2)}) copy-start(s32[8]{0:T(128)} %param.26) | copy-start | bytes 100
  1129.7 5.1 copy-start.16
  1129.7 7.2 slice-start.2
  1134.8 3.5 slice-start.3
  (18 other events, 40.4 us)
Sparse Core Ops, SparseCore 0:
  11.9 37.7 all-reduce.4
  53.5 80.3 all-gather.5
  153.4 75.2 reduce-scatter.4
  234.7 81.2 all-gather.7
  318.0 79.2 all-gather.9
  419.2 143.0 reduce-scatter.8
  569.6 81.3 all-gather.11
  686.1 75.2 reduce-scatter.10
  764.3 77.2 reduce-scatter.6
  868.3 255.4 all-reduce.6
where the time goes:
time: 1160 us; the launch traced here: 1150 us
  waiting for transfers between devices  862 us (74%)
  matrix products  133 us (11%)
  local copies, waits for them, and re-layouts  60.8 us (5%)
  blocking collectives  39.4 us (3%)
  other arithmetic  38.9 us (3%)
  between operations  14.9 us (1%)
    psum x1, waiting for transfers between devices, per_device(): lax.psum((w_qkv_grad, w_out_grad, w_up_grad, w_down_grad, w_mod_grad, b_m...  216 us
    reduce_scatter x1, waiting for transfers between devices, per_device(): lax.psum_scatter(jnp.einsum('wtf,df->wtd', row_block, w_up, preferred_ele...  143 us
    all_gather x1, waiting for transfers between devices, per_device(): d_branch_all = lax.all_gather(d_branch, 'mp', axis=0, tiled=True)  81.5 us
    all_gather x1, waiting for transfers between devices, per_device(): gathered_mlp = lax.all_gather(normed_mlp, 'mp', axis=0, tiled=True)  78.7 us
    reduce_scatter x1, waiting for transfers between devices, per_device(): lax.psum_scatter(jnp.einsum('wte,ed->wtd', row_block, w_out, preferred_el...  75.4 us
    reduce_scatter x1, waiting for transfers between devices, per_device(): lax.psum_scatter(jnp.einsum('wtf,fd->wtd', row_block, w_down, preferred_e...  74 us
    all_gather x1, waiting for transfers between devices, per_device(): d_mlp_all = lax.all_gather(d_mlp, 'mp', axis=0, tiled=True)  70.4 us
    all_gather x1, waiting for transfers between devices, per_device(): gathered_attn = lax.all_gather(normed_attn, 'mp', axis=0, tiled=True)  55 us
  transfers between devices with their start and end apart: 10, of which 10 were waited for; matrix products, arithmetic and copies ran while one was open for 9% of the time, Pallas kernels for 0%

commit v1 on v0

--- a/solution.py
+++ b/solution.py
@@ -145,8 +145,11 @@
     grad_rows = jnp.where(keep_rows, cotangent.astype(jnp.float32), 0.0)
     d_gate_mlp = jnp.sum(grad_rows * mlp_out, axis=1)
     d_mlp = (gate_mlp * grad_rows).astype(jnp.bfloat16)
-    d_mlp_all = lax.all_gather(d_mlp, "mp", axis=0, tiled=True)
-    normed_again = lax.all_gather(normed_mlp, "mp", axis=0, tiled=True)
+    d_mlp_all, normed_again = jnp.split(
+        lax.all_gather(jnp.concatenate([d_mlp, normed_mlp], axis=1), "mp", axis=0, tiled=True),
+        [d_mlp.shape[1]],
+        axis=1,
+    )
     pre_again = jnp.einsum("wtd,df->wtf", normed_again, w_up, preferred_element_type=jnp.float32)
     act_again = gelu_tanh(pre_again).astype(jnp.bfloat16)
     w_down_grad = jnp.einsum(

time: 1160 us -> 1210 us (1.043)
  waiting for transfers between devices: 862 us -> 897 us
    all_gather x1, waiting for transfers between devices: 70.4 us -> 150 us  [per_device(): lax.all_gather(jnp.concatenate([d_mlp, normed_mlp], axis=1), 'mp', axis=0...]
    all_gather x1, waiting for transfers between devices: 78.7 us -> 37.3 us  [per_device(): gathered_mlp = lax.all_gather(normed_mlp, 'mp', axis=0, tiled=True)]
    unnamed x93 -> x119, local copies, waits for them, and re-layouts: 28.4 us -> 29.6 us
  transfers between devices with their start and end apart: 10 -> 10, of which waited for: 10 -> 10; matrix products, arithmetic and copies ran while one was open for 9% -> 12% of each run, Pallas kernels for 0% -> 0%
where the time goes in v1:
time: 1210 us; the launch traced here: 1200 us
  waiting for transfers between devices  897 us (74%)
  matrix products  141 us (12%)
  local copies, waits for them, and re-layouts  62.4 us (5%)
  other arithmetic  44 us (4%)
  blocking collectives  39.5 us (3%)
  between operations  15 us (1%)
    psum x1, waiting for transfers between devices, per_device(): lax.psum((w_qkv_grad, w_out_grad, w_up_grad, w_down_grad, w_mod_grad, b_m...  215 us
    all_gather x1, waiting for transfers between devices, per_device(): lax.all_gather(jnp.concatenate([d_mlp, normed_mlp], axis=1), 'mp', axis=0...  150 us
    reduce_scatter x1, waiting for transfers between devices, per_device(): lax.psum_scatter(jnp.einsum('wtf,df->wtd', row_block, w_up, preferred_ele...  143 us
    all_gather x1, waiting for transfers between devices, per_device(): d_branch_all = lax.all_gather(d_branch, 'mp', axis=0, tiled=True)  80.7 us
    reduce_scatter x1, waiting for transfers between devices, per_device(): lax.psum_scatter(jnp.einsum('wtf,fd->wtd', row_block, w_down, preferred_e...  73.9 us
    reduce_scatter x1, waiting for transfers between devices, per_device(): lax.psum_scatter(jnp.einsum('wte,ed->wtd', row_block, w_out, preferred_el...  72.9 us
    all_gather x1, waiting for transfers between devices, per_device(): gathered_attn = lax.all_gather(normed_attn, 'mp', axis=0, tiled=True)  55 us
    all_gather x1, waiting for transfers between devices, per_device(): gathered_mlp = lax.all_gather(normed_mlp, 'mp', axis=0, tiled=True)  37.3 us
  transfers between devices with their start and end apart: 10, of which 10 were waited for; matrix products, arithmetic and copies ran while one was open for 12% of the time, Pallas kernels for 0%

profile of v1, /device:TPU:0, one launch (start us, length us, event | category | flops | bytes accessed | tf_op | source)
XLA Modules:
  0.0 1199.5 jit_solution(9052349754453714858)
XLA Ops:
  15.6 34.7 %all-reduce.5.cloned.1.call-done = f32[8,6,1024]{2,0,1:T(8,128)} async-done(((f32[8,6,1024]{2,0,1:T(8,128)}), f32[8,6,1024]{2,0,1:T(8,128)}) %all-reduce.5.cloned.1.call-update) | async-done | bytes 196624 | tf_op jit(solution)/shard_map/psum | solution.py:86
  55.4 5.7 convolution_bitcast_fusion
  61.0 12.1 %copy.103 = f32[4,16,16,16,16]{2,1,4,3,0:T(8,128)} copy(f32[4,16,16,16,16]{3,4,1,0,2:T(8,128)} %convolution_bitcast_fusion) | data formatting | bytes 2097152 | tf_op jit(solution)/shard_map/add | solution.py:49
  73.1 7.0 reshape.213
  80.2 55.0 %all-gather.6.cloned.1.call-done = bf16[8,256,1024]{2,1,0:T(8,128)(2,1)} async-done(((bf16[2,256,1024]{2,1,0:T(8,128)(2,1)}), bf16[8,256,1024]{2,1,0:T(8,128)(2,1)}) %all-gather.6.cloned.1.call-update) | async-done | bytes 4194320 | tf_op jit(solution)/shard_map/all_gather | solution.py:104
  135.1 6.1 convert_bitcast_fusion
  157.1 72.9 %reduce-scatter.5.cloned.1.call-done = bf16[2,256,1024]{2,1,0:T(8,128)(2,1)} async-done(((bf16[8,256,1024]{2,1,0:T(8,128)(2,1)}), bf16[2,256,1024]{2,1,0:T(8,128)(2,1)}) %reduce-scatter.5.cloned.1.call-update) | async-done | bytes 1048592 | tf_op jit(solution)/shard_map/reduce_scatter | solution.py:122
  238.9 150.2 %all-gather.10.cloned.1.call-done = bf16[8,512,1024]{2,1,0:T(8,128)(2,1)} async-done(((bf16[2,512,1024]{2,1,0:T(8,128)(2,1)}), bf16[8,512,1024]{2,1,0:T(8,128)(2,1)}) %all-gather.10.cloned.1.call-update) | async-done | bytes 8388624 | tf_op jit(solution)/shard_map/all_gather | solution.py:149
  389.1 10.8 fusion.29
  399.9 11.3 fusion.6
  413.2 6.8 fusion.62
  420.1 142.9 %reduce-scatter.9.cloned.1.call-done = f32[2,256,1024]{2,1,0:T(8,128)} async-done(((f32[8,256,1024]{2,1,0:T(8,128)}), f32[2,256,1024]{2,1,0:T(8,128)}) %reduce-scatter.9.cloned.1.call-update) | async-done | bytes 2097168 | tf_op jit(solution)/shard_map/reduce_scatter | solution.py:164
  571.0 80.7 %all-gather.12.cloned.1.call-done = bf16[8,256,1024]{2,1,0:T(8,128)(2,1)} async-done(((bf16[2,256,1024]{2,1,0:T(8,128)(2,1)}), bf16[8,256,1024]{2,1,0:T(8,128)(2,1)}) %all-gather.12.cloned.1.call-update) | async-done | bytes 4194320 | tf_op jit(solution)/shard_map/all_gather | solution.py:175
  655.3 6.3 convolution_convert_fusion.1
  664.1 6.1 multiply_reduce_fusion
  670.2 6.0 convert_reduce_fusion
  680.8 4.9 multiply_convert_fusion.5
  687.9 7.9 bitcast_convert_fusion
  695.8 37.3 %all-gather.8.cloned.1.call-done = bf16[8,256,1024]{2,1,0:T(8,128)(2,1)} async-done(((bf16[2,256,1024]{2,1,0:T(8,128)(2,1)}), bf16[8,256,1024]{2,1,0:T(8,128)(2,1)}) %all-gather.8.cloned.1.call-update) | async-done | bytes 4194320 | tf_op jit(solution)/shard_map/all_gather | solution.py:132
  733.1 13.4 %fusion.37 = bf16[8,256,1024]{2,1,0:T(8,128)(2,1)} fusion(bf16[1024,1024]{1,0:T(8,128)(2,1)} %param.19, bf16[8,256,1024]{2,1,0:T(8,128)(2,1)} %all-gather.8.cloned.1.call-done, bf16[1024,1024]{1,0:T(8,128)(2,1)} %param.18), kind=kOutput, calls=%fused_computation.55 | convolution fusion | flops 8610906112 | bytes 12582912 | tf_op jit(solution)/shard_map/wtf,fd->wtd/dot_general | solution.py:137
  747.0 10.0 fusion.44
  757.0 12.2 %fusion.47 = f32[1024,1024]{1,0:T(8,128)} fusion(bf16[8,512,1024]{2,1,0:T(8,128)(2,1)} %all-gather.10.cloned.1.call-done, f32[8,256,1024]{2,1,0:T(8,128)} %fusion.29), kind=kOutput, calls=%fused_computation.66 | convolution fusion | flops 4313841664 | bytes 16777216 | tf_op jit(solution)/shard_map/wtf,wtd->fd/dot_general | solution.py:155
  772.8 5.4 fusion.67
  778.3 33.0 %reduce-scatter.11.cloned.1.call-done = bf16[2,256,1024]{2,1,0:T(8,128)(2,1)} async-done(((bf16[8,256,1024]{2,1,0:T(8,128)(2,1)}), bf16[2,256,1024]{2,1,0:T(8,128)(2,1)}) %reduce-scatter.11.cloned.1.call-update) | async-done | bytes 1048592 | tf_op jit(solution)/shard_map/reduce_scatter | solution.py:216
  817.6 73.9 %reduce-scatter.7.cloned.1.call-done = bf16[2,256,1024]{2,1,0:T(8,128)(2,1)} async-done(((bf16[8,256,1024]{2,1,0:T(8,128)(2,1)}), bf16[2,256,1024]{2,1,0:T(8,128)(2,1)}) %reduce-scatter.7.cloned.1.call-update) | async-done | bytes 1048592 | tf_op jit(solution)/shard_map/reduce_scatter | solution.py:136
  891.5 5.2 fusion.56
  896.8 13.8 %all-gather = bf16[4,2,6144]{2,1,0:T(2,128)(2,1)S(1)} all-gather(bf16[1,2,6144]{2,1,0:T(2,128)(2,1)S(1)} %bitcast.179), channel_id=1, replica_groups=mesh['dp'=8,'mp'=4] {'mp'}, dimensions={0}, use_global_device_ids=true | all-gather | bytes 122880 | tf_op jit(solution)/shard_map/all_gather | solution.py:238
  918.8 6.2 reshape.189
  925.0 6.8 convolution_bitcast_fusion.3
  932.6 25.7 %all-reduce = (f32[6,1024]{1,0:T(8,128)}, f32[4,961]{1,0:T(4,128)}) all-reduce(f32[6,1024]{1,0:T(8,128)S(1)} %reshape.188, f32[4,961]{1,0:T(4,128)S(1)} %reshape.190), channel_id=1, replica_groups=mesh['dp'=8,'mp'=4] {'dp'}, use_global_device_ids=true, to_apply=%region_28.29 | all-reduce | flops 9988 | bytes 79904 | tf_op jit(solution)/shard_map/psum | solution.py:257
  958.2 215.5 %all-reduce.7.cloned.1.call-done = (f32[3,1024,256]{1,2,0:T(8,128)}, f32[256,1024]{1,0:T(8,128)}, f32[1024,1024]{1,0:T(8,128)}, f32[1024,1024]{1,0:T(8,128)}, f3...) async-done(((f32[3,1024,256]{1,2,0:T(8,128)}, f32[256,1024]{1,0:T(8,128)}, f32[1024,1024]{1,0:T(8,128)}, f32[1024,1024]{1,0:T(8,128)}, ...) | async-done | bytes 20160528 | tf_op jit(solution)/shard_map/psum | solution.py:257
  1179.6 5.1 copy.125
  (198 shorter events, 93.9 us)
Async XLA Ops:
  7.2 43.1 %all-reduce.5.cloned.1.call-start = ((), (), s32[]{:S(2)}) async-start(), calls=%async_computation.4 | async-start | bytes 393216 | tf_op jit(solution)/shard_map/psum | solution.py:86
  8.2 7.3 copy-start.41
  12.3 42.3 %copy-start.42 = (bf16[4,961]{1,0:T(4,128)(2,1)S(1)}, bf16[4,961]{1,0:T(4,128)(2,1)}, u32[]{:S(2)}) copy-start(bf16[4,961]{1,0:T(4,128)(2,1)} %param.24) | copy-start | bytes 23068
  12.4 122.8 %all-gather.6.cloned.1.call-start = ((), (), s32[]{:S(2)}) async-start(), calls=%async_computation.5 | async-start | bytes 5242880 | tf_op jit(solution)/shard_map/all_gather | solution.py:104
  13.9 47.2 %copy-start.31 = (f32[2,256]{1,0:T(2,128)}, f32[2,256]{1,0:T(2,128)S(1)}, u32[]{:S(2)}) copy-start(f32[2,256]{1,0:T(2,128)S(1)} %broadcast_multiply_fusion.1) | copy-start | bytes 6148
  15.5 34.8 %copy-start.39 = (f32[2,256]{1,0:T(2,128)}, f32[2,256]{1,0:T(2,128)S(1)}, u32[]{:S(2)}) copy-start(f32[2,256]{1,0:T(2,128)S(1)} %fusion.58) | copy-start | bytes 6148
  15.6 45.5 %copy-start.33 = (f32[2,256]{1,0:T(2,128)}, f32[2,256]{1,0:T(2,128)S(1)}, u32[]{:S(2)}) copy-start(f32[2,256]{1,0:T(2,128)S(1)} %fusion.106) | copy-start | bytes 6148
  54.6 175.4 %reduce-scatter.5.cloned.1.call-start = ((), (), s32[]{:S(2)}) async-start(), calls=%async_computation.6 | async-start | bytes 5242880 | tf_op jit(solution)/shard_map/reduce_scatter | solution.py:122
  73.1 7.0 copy-start.44
  154.5 234.6 %all-gather.10.cloned.1.call-start = ((), (), s32[]{:S(2)}) async-start(), calls=%async_computation.9 | async-start | bytes 10485760 | tf_op jit(solution)/shard_map/all_gather | solution.py:149
  238.9 324.1 %reduce-scatter.9.cloned.1.call-start = ((), (), s32[]{:S(2)}) async-start(), calls=%async_computation.10 | async-start | bytes 10485760 | tf_op jit(solution)/shard_map/reduce_scatter | solution.py:164
  389.1 10.8 copy-start.45
  389.1 10.8 copy-start.49
  399.9 13.3 %copy-start.48 = (bf16[1024,1024]{1,0:T(8,128)(2,1)S(1)}, bf16[1024,1024]{1,0:T(8,128)(2,1)}, u32[]{:S(2)}) copy-start(bf16[1024,1024]{1,0:T(8,128)(2,1)} %param.18) | copy-start | bytes 6291460
  420.0 231.7 %all-gather.12.cloned.1.call-start = ((), (), s32[]{:S(2)}) async-start(), calls=%async_computation.11 | async-start | bytes 5242880 | tf_op jit(solution)/shard_map/all_gather | solution.py:175
  570.2 162.9 %all-gather.8.cloned.1.call-start = ((), (), s32[]{:S(2)}) async-start(), calls=%async_computation.7 | async-start | bytes 5242880 | tf_op jit(solution)/shard_map/all_gather | solution.py:132
  570.9 240.3 %reduce-scatter.11.cloned.1.call-start = ((), (), s32[]{:S(2)}) async-start(), calls=%async_computation.12 | async-start | bytes 5242880 | tf_op jit(solution)/shard_map/reduce_scatter | solution.py:216
  655.3 6.3 copy-start.15
  670.2 6.0 copy-start.9
  695.8 195.7 %reduce-scatter.7.cloned.1.call-start = ((), (), s32[]{:S(2)}) async-start(), calls=%async_computation.8 | async-start | bytes 5242880 | tf_op jit(solution)/shard_map/reduce_scatter | solution.py:136
  746.5 427.2 %all-reduce.7.cloned.1.call-start = ((), (), s32[]{:S(2)}) async-start(), calls=%async_computation.13 | async-start | bytes 40321024 | tf_op jit(solution)/shard_map/psum | solution.py:257
  757.0 12.2 %copy-start.18 = (bf16[8,4,64,256]{3,2,1,0:T(8,128)(2,1)S(1)}, bf16[8,4,64,256]{3,2,1,0:T(8,128)(2,1)}, u32[]{:S(2)}) copy-start(bf16[8,4,64,256]{3,2,1,0:T(8,128)(2,1)} %copy-done.17) | copy-start | bytes 3145732
  757.0 12.2 %copy-start.47 = (bf16[8,256,1024]{2,1,0:T(8,128)(2,1)S(1)}, bf16[8,256,1024]{2,1,0:T(8,128)(2,1)}, u32[]{:S(2)}) copy-start(bf16[8,256,1024]{2,1,0:T(8,128)(2,1)} %all-gather.12.cloned.1.call-done) | copy-start | bytes 12582916
  772.8 39.9 %copy-start.26 = (f32[2,1024]{1,0:T(2,128)S(1)}, f32[2,1024]{1,0:T(2,128)}, u32[]{:S(2)}) copy-start(f32[2,1024]{1,0:T(2,128)} %copy-done.25) | copy-start | bytes 24580
  772.8 39.9 %copy-start.32 = (f32[2,256]{1,0:T(2,128)S(1)}, f32[2,256]{1,0:T(2,128)}, u32[]{:S(2)}) copy-start(f32[2,256]{1,0:T(2,128)} %copy-done.31) | copy-start | bytes 6148
  778.3 36.6 %copy-start.40 = (f32[2,256]{1,0:T(2,128)S(1)}, f32[2,256]{1,0:T(2,128)}, u32[]{:S(2)}) copy-start(f32[2,256]{1,0:T(2,128)} %copy-done.39) | copy-start | bytes 6148
  778.3 36.6 %copy-start.34 = (f32[2,256]{1,0:T(2,128)S(1)}, f32[2,256]{1,0:T(2,128)}, u32[]{:S(2)}) copy-start(f32[2,256]{1,0:T(2,128)} %copy-done.33) | copy-start | bytes 6148
  896.7 14.9 %copy-start.30 = (f32[8,256]{1,0:T(8,128)S(1)}, f32[8,256]{1,0:T(8,128)}, u32[]{:S(2)}) copy-start(f32[8,256]{1,0:T(8,128)} %copy-done.29) | copy-start | bytes 24580
  896.7 14.9 %copy-start.36 = (bf16[8,128]{1,0:T(8,128)(2,1)S(1)}, bf16[8,128]{1,0:T(8,128)(2,1)}, u32[]{:S(2)}) copy-start(bf16[8,128]{1,0:T(8,128)(2,1)} %copy-done.35) | copy-start | bytes 6148
  896.7 14.9 %copy-start.38 = (bf16[8,128]{1,0:T(8,128)(2,1)S(1)}, bf16[8,128]{1,0:T(8,128)(2,1)}, u32[]{:S(2)}) copy-start(bf16[8,128]{1,0:T(8,128)(2,1)} %copy-done.37) | copy-start | bytes 6148
  896.7 15.9 %copy-start.43 = (s32[8]{0:T(128)S(1)}, s32[8]{0:T(128)}, u32[]{:S(2)}) copy-start(s32[8]{0:T(128)} %param.26) | copy-start | bytes 100
  1179.6 7.2 slice-start
  (31 other events, 82.4 us)
Sparse Core Ops, SparseCore 0:
  12.5 37.7 all-reduce.4
  54.7 80.3 all-gather.5
  154.6 75.2 reduce-scatter.4
  239.0 150.1 all-gather.9
  420.2 142.7 reduce-scatter.8
  570.3 81.3 all-gather.11
  653.9 79.2 all-gather.7
  736.0 75.2 reduce-scatter.10
  814.2 77.2 reduce-scatter.6
  918.2 255.4 all-reduce.6
